TPU v7x, 32 devices: a whole 2x2x4 slice. The times are simulated.
32 devices in a mesh: grp: 2 (over x), feat: 16 (over z, y, core).
Axes of the slice: x: 2, y: 2, z: 4, core: 2. Of those that a mesh axis runs over, the one named last changes fastest.
Arguments:
- x_acts: bfloat16 [8, 1024, 4096], P('grp'), parts along dimension 0, may hold values from -6 to 6
- delta: bfloat16 [8, 1024, 4096], P('grp', None, 'feat'), parts along dimension 0, may hold values from -6 to 6
- pattern: int32 [32, 32], replicated, may hold values 0 or 1
- row_signs: int32 [4096], replicated, may hold values from -1 to 1, as said below
- col_signs: int32 [4096], replicated, may hold values from -1 to 1, as said below
- cols: int32 [8192], replicated, may hold values from 0 to 16777215
Outputs:
- sketch: float32 [8, 8192], P('grp'), parts along dimension 0
There are 2 independent parts, one for each index of `grp`. A program takes and returns all parts, laid end to end along the dimension named above; an argument that names none is the same for every part. Nothing has to cross between parts.
Inputs may be any that keep to these rules, and one draw needn't show every extreme that they name: `row_signs`: every entry is -1 or +1. `col_signs`: every entry is -1 or +1.
All inputs are finite; a program needn't handle non-finite values.
Results may differ from a plain program's by a relative error of at most 0.0029.
Values may be sent and summed in bfloat16 or wider, within the bound.
No kernel may reach another device: no remote copies, remote signals or barrier semaphores. Data moves between devices by JAX's collectives and lax.ppermute only.
A program may use at most 192 MiB of HBM per device.

v0:
```python
import math

import jax
import jax.numpy as jnp
from jax import lax
from jax.sharding import PartitionSpec as P

BLK = 128
SKETCH = 8192


def partner(value, axis, apart):
    mask = 2**apart
    pairs = [(source, source ^ mask) for source in range(lax.axis_size(axis))]
    return lax.ppermute(value, axis, pairs)


def hadamard(mat_order):
    row_ids = lax.iota(jnp.int32, mat_order)[:, None]
    col_ids = lax.iota(jnp.int32, mat_order)[None, :]
    intersection = row_ids & col_ids
    parity = jnp.zeros((mat_order, mat_order), jnp.int32)
    for bit_pos in range(max(mat_order - 1, 0).bit_length()):
        parity = parity ^ intersection >> bit_pos & 1
    return (1 - 2 * parity).astype(jnp.float32)


def parity_sign(left_ids, right_ids, n_bits):
    intersection = left_ids & right_ids
    parity = jnp.zeros_like(intersection)
    for bit_pos in range(n_bits):
        parity = parity ^ intersection >> bit_pos & 1
    return (1 - 2 * parity).astype(jnp.float32)


def build_mask(global_rows, pattern, width_in):
    row_select = (
        (global_rows // BLK)[:, None] == lax.iota(jnp.int32, pattern.shape[0])[None, :]
    ).astype(jnp.float32)
    col_block = lax.iota(jnp.int32, width_in) // BLK
    col_select = (lax.iota(jnp.int32, pattern.shape[1])[:, None] == col_block[None, :]).astype(
        jnp.float32
    )
    return jnp.dot(jnp.dot(row_select, pattern.astype(jnp.float32)), col_select)


def signed_gradient(delta_part, acts_part, global_rows, sign_rows, pattern, col_signs):
    tokens_each = acts_part.shape[1]
    width_in = acts_part.shape[2]
    block_mask = build_mask(global_rows, pattern, width_in)
    gradient = (
        jnp.einsum("etr,etc->erc", delta_part, acts_part, preferred_element_type=jnp.float32)
        / tokens_each
    )
    gradient = (gradient * block_mask[None]).astype(jnp.bfloat16)
    sign_table = (sign_rows[:, None] * col_signs[None, :]).astype(jnp.bfloat16)
    return gradient * sign_table[None]


def column_section(signed):
    examples, rows_here, width_in = signed.shape
    low_width = min(128, width_in)
    high_width = width_in // low_width
    shaped = signed.reshape(examples, rows_here, high_width, low_width)
    section = jnp.einsum(
        "erqj,jk->erqk",
        shaped,
        hadamard(low_width).astype(jnp.bfloat16),
        preferred_element_type=jnp.float32,
    )
    section = jnp.einsum(
        "erqk,qp->pker", section, hadamard(high_width), precision=lax.Precision.HIGHEST
    )
    return section.reshape(width_in, examples, rows_here)


def kept_entries(section, global_rows, cols, width_in, width_out):
    row_bits = max(width_out - 1, 0).bit_length()
    weight = parity_sign(global_rows[:, None], (cols // width_in)[None, :], row_bits)
    picked = jnp.take(section, cols % width_in, axis=0)
    return jnp.einsum("ker,rk->ek", picked, weight, precision=lax.Precision.HIGHEST)


def per_device(x_acts, delta, pattern, row_signs, col_signs, cols):
    examples, tokens_each, width_in = x_acts.shape
    local_rows = delta.shape[2]
    feat_count = lax.axis_size("feat")
    my_index = lax.axis_index("feat")
    width_out = local_rows * feat_count
    group_size = max(feat_count // examples, 1)
    held = max(examples // feat_count, 1)
    sub_rows = local_rows // group_size
    pieces = delta.reshape(examples, tokens_each, group_size, sub_rows)
    pieces = pieces.transpose(0, 2, 1, 3).reshape(examples * group_size, tokens_each, sub_rows)
    regrouped = lax.all_to_all(pieces, "feat", split_axis=0, concat_axis=2, tiled=True)
    slot = my_index % group_size
    first_example = my_index // group_size * held
    acts_mine = lax.dynamic_slice_in_dim(x_acts, first_example, held, 0)
    position = lax.iota(jnp.int32, feat_count * sub_rows)
    global_rows = position // sub_rows * local_rows + slot * sub_rows + position % sub_rows
    sign_rows = jnp.take(row_signs, global_rows)
    signed = signed_gradient(regrouped, acts_mine, global_rows, sign_rows, pattern, col_signs)
    section = column_section(signed)
    partial_value = kept_entries(section, global_rows, cols, width_in, width_out)
    for bit_pos in range(max(group_size - 1, 0).bit_length()):
        partial_value = partial_value + partner(partial_value, "feat", bit_pos)
    part_len = SKETCH // group_size
    mine = lax.dynamic_slice_in_dim(partial_value, slot * part_len, part_len, 1)
    gathered = lax.all_gather(mine[None], "feat", axis=0, tiled=True)
    total = gathered.reshape(feat_count // group_size, group_size, held, part_len)
    total = total.transpose(0, 2, 1, 3).reshape(examples, SKETCH)
    return total / math.sqrt(SKETCH)


def solution(mesh):
    placed = (P("grp", None, None), P("grp", None, "feat"), P(), P(), P(), P())
    return jax.shard_map(
        per_device, mesh=mesh, in_specs=placed, out_specs=P("grp", None), check_vma=False
    )
```

profile of v0, /device:TPU:0, one launch (start us, length us, event | category | flops | bytes accessed | tf_op | source)
XLA Modules:
  0.0 283.9 jit_solution(2217800679359277054)
XLA Ops:
  0.0 0.0 copy-start
  0.0 2.9 %fusion.111 = (bf16[4,1024,64]{2,1,0:T(8,128)(2,1)S(1)}, bf16[4,1024,64]{2,1,0:T(8,128)(2,1)S(1)}, bf16[4,1024,64]{2,1,0:T(8,128)(2,1)S(1)}, bf16[4,1024,64]{2,1,0:T(8,128)(2,1)S(1)}) fusion(bf16[4,1024,256]{2,1,0:T(8,128)(2,1)} %param.7), kind=kLoop, calls=%fused_computation.160 | loop fusion | bytes 4194304 | tf_op jit(solution)/shard_map/slice
  3.0 2.4 pad_maximum_fusion
  5.3 4.8 %copy.13 = bf16[16,1024,64]{1,2,0:T(8,128)(2,1)} copy(bf16[16,1024,64]{2,1,0:T(8,128)(2,1)} %bitcast.36) | data formatting | bytes 4194304 | tf_op jit(solution)/shard_map/reshape | solution.py:94
  10.1 7.4 %all-to-all-start = ((bf16[16,1024,64]{1,2,0:T(8,128)(2,1)}), bf16[16,1024,64]{1,2,0:T(8,128)(2,1)S(1)}, u32[]{:S(2)}, u32[]{:S(2)}) async-start(bf16[16,1024,64]{1,2,0:T(8,128)(2,1)} %copy.13), calls=%async_computation | async-start | bytes 4194304 | tf_op jit(solution)/shard_map/all_to_all | solution.py:95
  17.5 0.8 broadcast_clamp_fusion
  18.4 43.8 %fusion.15 = f32[8192,1024]{0,1:T(8,128)} fusion(s32[8192]{0:T(1024)S(1)} %get-tuple-element.10, s32[1024]{0:T(1024)S(1)} %fusion.92), kind=kLoop, calls=%fused_computation.29 | loop fusion | flops 327155712 | bytes 33591296
  62.2 0.0 copy-start.2
  62.2 0.0 copy-start.3
  62.2 0.0 copy-start.4
  62.2 33.5 %copy.19 = f32[8192,1024]{1,0:T(8,128)} copy(f32[8192,1024]{0,1:T(8,128)} %fusion.15) | data formatting | bytes 67108864
  95.7 0.0 copy-done
  95.7 6.2 %gather_fusion = s32[1024]{0:T(1024)S(1)} fusion(s32[4096]{0:T(1024)S(1)} %copy-done, s32[1024]{0:T(1024)S(1)} %broadcast_clamp_fusion.1), kind=kCustom, calls=%fused_computation | custom fusion | bytes 12288 | tf_op jit(solution)/shard_map/jit(_take)/gather | solution.py:101
  101.9 0.0 copy-done.2
  102.0 0.0 copy-done.3
  102.0 7.3 %fusion.33 = f32[1024,4096]{1,0:T(8,128)} fusion(s32[4096]{0:T(1024)S(1)} %add_select_fusion.2, s32[1024]{0:T(1024)S(1)} %get-tuple-element.11, s32[32,32]{1,0:T(8,128)S(1)} %copy-done.3), kind=kOutput, calls=%fused_computation.50 | convolution fusion | flops 270697472 | bytes 16801792 | tf_op jit(solution)/shard_map/dot_general | solution.py:44
  109.3 0.0 all-to-all-done
  109.3 0.0 copy-done.4
  109.3 16.8 %fusion.28 = bf16[128,8,32,128]{3,1,2,0:T(8,128)(2,1)} fusion(s32[4096]{0:T(1024)S(1)} %copy-done.4, s32[1024]{0:T(1024)S(1)} %get-tuple-element.12, f32[1024,4096]{1,0:T(8,128)} %fusion.33, bf16[1024,1024]{0,1:T(8,128)(2,1)S(1)} %bitcast.37, bf16[4,1024,4096]{2,1,0:T(8,128)(2,1)} %param.6, s32[]{:T(128)S(6)} %select_n.139), kind=kOutput, calls=%fused_computation.46 | convolution fusion | flops 8615100416 | bytes 35672068 | tf_op jit(solution)/shard_map/etr,etc->erc/dot_general | solution.py:52
  126.1 9.4 %copy.23 = bf16[128,8,32,128]{3,2,1,0:T(8,128)(2,1)} copy(bf16[128,8,32,128]{3,1,2,0:T(8,128)(2,1)} %fusion.28) | data formatting | bytes 16777216
  135.5 11.5 %fusion.40 = f32[1024,32,128]{2,1,0:T(8,128)} fusion(bf16[1024,32,128]{2,1,0:T(8,128)(2,1)} %bitcast.35), kind=kOutput, calls=%fused_computation.65 | convolution fusion | flops 1074151424 | bytes 25165824 | tf_op jit(solution)/shard_map/erqj,jk->erqk/dot_general | solution.py:65
  147.0 21.4 %convolution_bitcast_fusion = f32[32,128,1,1024]{1,0,3,2:T(8,128)} fusion(f32[1024,32,128]{2,1,0:T(8,128)} %fusion.40), kind=kOutput, calls=%fused_computation.44 | convolution fusion | flops 1610631168 | bytes 33554432 | tf_op jit(solution)/shard_map/erqk,qp->pker/dot_general | solution.py:71
  168.4 16.5 %copy.22 = f32[32,128,1,1024]{3,1,0,2:T(8,128)} copy(f32[32,128,1,1024]{1,0,3,2:T(8,128)} %convolution_bitcast_fusion) | data formatting | bytes 33554432 | tf_op jit(solution)/shard_map/reshape | solution.py:74
  185.0 0.0 copy-start.1
  185.0 49.4 %gather_fusion.1 = f32[8192,1024]{1,0:T(8,128)} fusion(f32[4096,1024]{1,0:T(8,128)} %bitcast.34, s32[8192]{0:T(1024)S(1)} %get-tuple-element.9), kind=kCustom, calls=%fused_computation.1 | custom fusion | bytes 67141632 | tf_op jit(solution)/shard_map/jit(_take)/gather | solution.py:80
  234.4 21.1 %multiply_reduce_fusion = f32[8192]{0:T(1024)S(1)} fusion(f32[8192,1024]{1,0:T(8,128)} %copy.19, f32[8192,1024]{1,0:T(8,128)} %gather_fusion.1, pred[8192]{0:T(1024)(128)(4,1)S(1)} %compare_and_fusion), kind=kLoop, calls=%fused_computation.41 | loop fusion | flops 25157632 | bytes 67149824 | tf_op jit(solution)/shard_map/ker,rk->ek/dot_general | solution.py:81
  255.4 0.5 collective-permute-start
  255.9 0.9 collective-permute-done
  256.8 1.9 collective-permute-start.1
  258.7 2.1 collective-permute-done.1
  260.8 22.0 %all-gather.1 = f32[16,1,2048]{2,1,0:T(1,128)S(1)} all-gather(f32[1,1,2048]{2,1,0:T(1,128)S(1)} %fusion.77), channel_id=2, replica_groups=mesh['grp'=2,'feat'=16] {'feat'}, dimensions={0}, use_global_device_ids=true | all-gather | bytes 139264 | tf_op jit(solution)/shard_map/all_gather | solution.py:109
  282.8 0.4 multiply_reduce_fusion.1
  283.2 0.7 div.85
  283.9 0.0 copy-done.1
  (8 shorter events, 0.1 us)
Async XLA Ops:
  0.0 95.7 %copy-start = (s32[4096]{0:T(1024)S(1)}, s32[4096]{0:T(1024)}, u32[]{:S(2)}) copy-start(s32[4096]{0:T(1024)} %param.9) | copy-start | bytes 49156
  10.1 99.2 %all-to-all-start = ((bf16[16,1024,64]{1,2,0:T(8,128)(2,1)}), bf16[16,1024,64]{1,2,0:T(8,128)(2,1)S(1)}, u32[]{:S(2)}, u32[]{:S(2)}) async-start(bf16[16,1024,64]{1,2,0:T(8,128)(2,1)} %copy.13), calls=%async_computation | async-start | bytes 4194304 | tf_op jit(solution)/shard_map/all_to_all | solution.py:95
  62.2 39.7 %copy-start.2 = (s32[8192]{0:T(1024)S(1)}, s32[8192]{0:T(1024)}, u32[]{:S(2)}) copy-start(s32[8192]{0:T(1024)} %param.11) | copy-start | bytes 98308
  62.2 39.8 %copy-start.3 = (s32[32,32]{1,0:T(8,128)S(1)}, s32[32,32]{1,0:T(8,128)}, u32[]{:S(2)}) copy-start(s32[32,32]{1,0:T(8,128)} %param.8) | copy-start | bytes 12292
  62.2 47.1 %copy-start.4 = (s32[4096]{0:T(1024)S(1)}, s32[4096]{0:T(1024)}, u32[]{:S(2)}) copy-start(s32[4096]{0:T(1024)} %param.10) | copy-start | bytes 49156
  185.0 98.9 %copy-start.1 = (s32[4096]{0:T(1024)S(1)}, s32[4096]{0:T(1024)}, u32[]{:S(2)}) copy-start(s32[4096]{0:T(1024)} %param.9) | copy-start | bytes 49156
  255.4 1.3 collective-permute-start
  256.8 4.0 %collective-permute-start.1 = (f32[1,8192]{1,0:T(1,128)S(1)}, f32[1,8192]{1,0:T(1,128)S(1)}, u32[]{:S(2)}, u32[]{:S(2)}) collective-permute-start(f32[1,8192]{1,0:T(1,128)S(1)} %add.176), channel_id=1, source_target_pairs={{0,2},{1,3},{2,0},{3,1},{4,6},{5,7},{6,4},{7,5},{8,10},{9,11},{10,... | collective-permute-start | bytes 98312 | tf_op jit(solution)/shard_map/ppermute | solution.py:15
where the time goes:
time: 285 us; the launch traced here: 284 us
  local copies, waits for them, and re-layouts  123 us (43%)
  other arithmetic  68.6 us (24%)
  matrix products  57 us (20%)
  blocking collectives  22 us (8%)
  starting transfers between devices  9.8 us (3%)
  waiting for transfers between devices  2.92 us (1%)
    gather x1, local copies, waits for them, and re-layouts, kept_entries(): picked = jnp.take(section, cols % width_in, axis=0)  49.4 us
    unnamed x2, other arithmetic  43.8 us
    unnamed x12, local copies, waits for them, and re-layouts  42.9 us
    all_gather x1, blocking collectives, per_device(): gathered = lax.all_gather(mine[None], 'feat', axis=0, tiled=True)  22 us
    dot_general x1, matrix products, column_section(): jnp.einsum('erqk,qp->pker', section, hadamard(high_width), precision=lax....  21.4 us
    dot_general x1, other arithmetic, kept_entries(): jnp.einsum('ker,rk->ek', picked, weight, precision=lax.Precision.HIGHEST)  21.1 us
    dot_general x1, matrix products, signed_gradient(): jnp.einsum('etr,etc->erc', delta_part, acts_part, preferred_element_type=...  16.8 us
    reshape x1, local copies, waits for them, and re-layouts, column_section(): return section.reshape(width_in, examples, rows_here)  16.5 us
  transfers between devices with their start and end apart: 3, of which 2 were waited for; matrix products, arithmetic and copies ran while one was open for 32% of the time, Pallas kernels for 0%

commit v1 on v0

v1 whole, which is shorter than its diff:
```python
import functools
import math

import jax
import jax.numpy as jnp
from jax import lax
from jax.experimental import pallas as pl
from jax.experimental.pallas import tpu as pltpu
from jax.sharding import PartitionSpec as P

BLK = 128
LANES = 128
SUBLANES = 8
CHUNK = 1024
VMEM_LIMIT = 60 * 2**20


def partner(value, axis, apart):
    mask = 2**apart
    pairs = [(source, source ^ mask) for source in range(lax.axis_size(axis))]
    return lax.ppermute(value, axis, pairs)


def parity(ids):
    for shift in (8, 4, 2, 1):
        ids = ids ^ (ids >> shift)
    return ids & 1


def transform_kernel(
    examples, free, n_blocks, tile_idx, sign_idx, x_ref, d_ref, factor_ref,
    mask_ref, rows_ref, out_ref, dt_ref, had_ref, sign_ref, s_ref, t_ref,
):
    example, chunk = pl.program_id(0), pl.program_id(1)
    last = (example == pl.num_programs(0) - 1) & (chunk == pl.num_programs(1) - 1)
    rows = d_ref.shape[2]
    width = x_ref.shape[2]
    blocks_here = width // LANES
    n_low = n_blocks // free
    row_blocks = mask_ref.shape[0]
    band = rows // row_blocks

    @pl.when((example == 0) & (chunk == 0))
    def _():
        left = lax.broadcasted_iota(jnp.int32, (rows, rows), 0)
        right = lax.broadcasted_iota(jnp.int32, (rows, rows), 1)
        had_ref[...] = (1 - 2 * parity(left & right)).astype(jnp.bfloat16)

        def signs(step, carry):
            base = step * (SUBLANES * SUBLANES)
            shape = (SUBLANES * SUBLANES, LANES)
            row = base + lax.broadcasted_iota(jnp.int32, shape, 0)
            lane = lax.broadcasted_iota(jnp.int32, shape, 1)
            entry = row // SUBLANES
            bit = row % SUBLANES // examples
            both = (entry % LANES & lane) ^ ((entry // LANES & bit) << 7)
            sign_ref[pl.ds(pl.multiple_of(base, SUBLANES * SUBLANES), shape[0]), :] = (
                1 - 2 * parity(both)
            ).astype(jnp.float32)
            return carry

        lax.fori_loop(0, free * LANES // SUBLANES, signs, 0)

    @pl.when(chunk == 0)
    def _():
        dt_ref[...] = (d_ref[0] * rows_ref[...]).T

    grad = jnp.dot(dt_ref[...], x_ref[0], preferred_element_type=jnp.float32)
    for b in range(row_blocks):
        part = slice(b * band, (b + 1) * band)
        s_ref[part, :] = (grad[part, :] * mask_ref[b : b + 1, :]).astype(jnp.bfloat16)
    out = jnp.dot(had_ref[...], s_ref[...], preferred_element_type=jnp.float32)
    for j in range(blocks_here):
        block = chunk * blocks_here + j
        start = (block % n_low) * rows * SUBLANES + block // n_low * examples + example
        t_ref[pl.ds(start, rows, stride=SUBLANES), :] = out[:, j * LANES : (j + 1) * LANES]

    @pl.when(last)
    def _():
        def butterfly(row, carry):
            tiles = [
                t_ref[pl.ds(pl.multiple_of((q * rows + row) * SUBLANES, SUBLANES), SUBLANES), :]
                for q in range(n_low)
            ]
            half = 1
            while half < n_low:
                tiles = [
                    tiles[q] + tiles[q + half] if q & half == 0 else tiles[q - half] - tiles[q]
                    for q in range(n_low)
                ]
                half *= 2
            for q in range(n_low):
                t_ref[pl.ds(pl.multiple_of((q * rows + row) * SUBLANES, SUBLANES), SUBLANES), :] = tiles[q]
            return carry

        lax.fori_loop(0, rows, butterfly, 0, unroll=2)

        lane = lax.broadcasted_iota(jnp.int32, (SUBLANES, LANES), 1)

        def term(group, first, count):
            if count == 1:
                k = group * LANES + first
                tile = pl.multiple_of(tile_idx[k], SUBLANES)
                sign = pl.multiple_of(sign_idx[k], SUBLANES)
                return t_ref[pl.ds(tile, SUBLANES), :] * sign_ref[pl.ds(sign, SUBLANES), :]
            half = count // 2
            left, right = term(group, first, half), term(group, first + half, half)
            low = lane & half == 0
            return jnp.where(low, left, right) + pltpu.roll(
                jnp.where(low, right, left), half, 1
            )

        def sample(group, carry):
            found = term(group, 0, LANES)
            total = found[:examples]
            for bit in range(1, free):
                total = total + found[bit * examples : (bit + 1) * examples]
            here = pl.ds(pl.multiple_of(group * LANES, LANES), LANES)
            out_ref[:, here] = total * factor_ref[pl.ds(group, 1), :]
            return carry

        lax.fori_loop(0, out_ref.shape[1] // LANES, sample, 0)


def transform(x_acts, delta, factor, mask, sign_rows, tile_idx, sign_idx):
    examples, tokens, width = x_acts.shape
    rows = delta.shape[2]
    n_kept = tile_idx.shape[0]
    free = SUBLANES // examples
    chunk = CHUNK
    whole = lambda shape: pl.BlockSpec(shape, lambda e, j, *_: (0,) * len(shape))
    kernel = functools.partial(transform_kernel, examples, free, width // LANES)
    return pl.pallas_call(
        kernel,
        out_shape=jax.ShapeDtypeStruct((examples, n_kept), jnp.float32),
        grid_spec=pltpu.PrefetchScalarGridSpec(
            num_scalar_prefetch=2,
            grid=(examples, width // chunk),
            in_specs=[
                pl.BlockSpec((1, tokens, chunk), lambda e, j, *_: (e, 0, j)),
                pl.BlockSpec((1, tokens, rows), lambda e, j, *_: (e, 0, 0)),
                whole(factor.shape),
                pl.BlockSpec((mask.shape[0], chunk), lambda e, j, *_: (0, j)),
                whole(sign_rows.shape),
            ],
            out_specs=whole((examples, n_kept)),
            scratch_shapes=[
                pltpu.VMEM((rows, tokens), jnp.bfloat16),
                pltpu.VMEM((rows, rows), jnp.bfloat16),
                pltpu.VMEM((free * LANES * SUBLANES, LANES), jnp.float32),
                pltpu.VMEM((rows, chunk), jnp.bfloat16),
                pltpu.VMEM((rows * width // LANES * examples, LANES), jnp.float32),
            ],
        ),
        compiler_params=pltpu.CompilerParams(vmem_limit_bytes=VMEM_LIMIT),
    )(tile_idx, sign_idx, x_acts, delta, factor, mask, sign_rows)


def per_device(x_acts, delta, pattern, row_signs, col_signs, cols):
    examples, tokens, width_in = x_acts.shape
    rows = delta.shape[2]
    n_kept = cols.shape[0]
    free = SUBLANES // examples
    n_low = width_in // LANES // free
    feat = lax.axis_size("feat")
    me = lax.axis_index("feat")

    first_row = me * rows
    row_blocks = max(rows // BLK, 1)
    here = lax.dynamic_slice_in_dim(pattern, first_row // BLK, row_blocks, 0)
    mask = (jnp.repeat(here, BLK, axis=1) * col_signs[None]).astype(jnp.float32)
    sign_rows = lax.dynamic_slice_in_dim(row_signs, first_row, rows, 0)
    sign_rows = sign_rows[None].astype(jnp.bfloat16)

    kept_row, kept_col = cols // width_in, cols % width_in
    block, lane = kept_col // LANES, kept_col % LANES
    tile_idx = (block % n_low * rows + kept_row % rows) * SUBLANES
    sign_idx = (block // n_low * LANES + lane) * SUBLANES
    factor = (1 - 2 * parity(kept_row // rows & me)).astype(jnp.float32)
    factor = (factor / (tokens * math.sqrt(n_kept))).reshape(n_kept // LANES, LANES)

    value = transform(x_acts, delta, factor, mask, sign_rows, tile_idx, sign_idx)

    bits = max(feat - 1, 0).bit_length()
    half = n_kept // 2
    low = me % 2 == 0
    mine = jnp.where(low, value[:, :half], value[:, half:])
    other = jnp.where(low, value[:, half:], value[:, :half])
    mine = mine + partner(other, "feat", 0)
    for bit in range(1, bits):
        mine = mine + partner(mine, "feat", bit)
    back = partner(mine, "feat", 0)
    return jnp.concatenate([jnp.where(low, mine, back), jnp.where(low, back, mine)], axis=1)


def solution(mesh):
    placed = (P("grp", None, None), P("grp", None, "feat"), P(), P(), P(), P())
    return jax.shard_map(
        per_device, mesh=mesh, in_specs=placed, out_specs=P("grp", None), check_vma=False
    )
```

time: 285 us -> 103 us (0.36)
  local copies, waits for them, and re-layouts: 123 us -> 0.66 us
  Pallas kernels: 0 us -> 76 us
  other arithmetic: 68.6 us -> 7.6 us
  matrix products: 57 us -> 0 us
  blocking collectives: 22 us -> 0 us
  waiting for transfers between devices: 2.92 us -> 9.16 us
    pallas_call x0 -> x1, Pallas kernels: none -> 76 us  [transform(): pl.pallas_call(kernel, out_shape=jax.ShapeDtypeStruct((examples, n_kept),...]
    dot_general x4 -> x0, matrix products: 57 us -> none  [the longest x1 21.4 us: column_section(): jnp.einsum('erqk,qp->pker', section, hadamard(high_width), precision=lax....]
    gather x2 -> x0, local copies, waits for them, and re-layouts: 55.5 us -> none  [the longest x1 49.4 us: kept_entries(): picked = jnp.take(section, cols % width_in, axis=0)]
    unnamed x2 -> x0, other arithmetic: 43.8 us -> none
    unnamed x12 -> x3, local copies, waits for them, and re-layouts: 42.9 us -> 0.08 us
    all_gather x1 -> x0, blocking collectives: 22 us -> none  [per_device(): gathered = lax.all_gather(mine[None], 'feat', axis=0, tiled=True)]
    reshape x2 -> x0, local copies, waits for them, and re-layouts: 21.3 us -> none  [the longest x1 16.5 us: column_section(): return section.reshape(width_in, examples, rows_here)]
    dot_general x1 -> x0, other arithmetic: 21.1 us -> none  [kept_entries(): jnp.einsum('ker,rk->ek', picked, weight, precision=lax.Precision.HIGHEST)]
  transfers between devices with their start and end apart: 3 -> 5, of which waited for: 2 -> 5; matrix products, arithmetic and copies ran while one was open for 32% -> 0% of each run, Pallas kernels for 0% -> 0%
where the time goes in v1:
time: 103 us; the launch traced here: 102 us
  Pallas kernels  76 us (74%)
  waiting for transfers between devices  9.16 us (9%)
  starting transfers between devices  8.52 us (8%)
  other arithmetic  7.6 us (7%)
    pallas_call x1, Pallas kernels, transform(): pl.pallas_call(kernel, out_shape=jax.ShapeDtypeStruct((examples, n_kept),...  76 us
    ppermute x5, waiting for transfers between devices, partner(): return lax.ppermute(value, axis, pairs)  9.16 us
    ppermute x5, starting transfers between devices, partner(): return lax.ppermute(value, axis, pairs)  8.52 us
  transfers between devices with their start and end apart: 5, of which 5 were waited for; matrix products, arithmetic and copies ran while one was open for 0% of the time, Pallas kernels for 0%

profile of v1, /device:TPU:0, one launch (start us, length us, event | category | flops | bytes accessed | tf_op | source)
XLA Modules:
  0.0 102.0 jit_solution(14625818394657832609)
XLA Ops:
  0.0 0.0 copy-start
  0.0 1.4 %fusion.13.factor_ref = f32[64,128]{1,0:T(8,128)} fusion(s32[]{:T(128)S(6)} %axis_index.12, s32[8192]{0:T(1024)} %param.11), kind=kLoop, calls=%fused_computation.45 | loop fusion | flops 360448 | bytes 65540 | tf_op jit(solution)/shard_map/reshape | solution.py:180
  1.4 1.5 %fusion.5 = (s32[8192]{0:T(1024)}, s32[8192]{0:T(1024)}) fusion(s32[8192]{0:T(1024)} %param.11), kind=kLoop, calls=%fused_computation.32 | loop fusion | flops 606208 | bytes 98304 | tf_op jit(solution)/shard_map/mul | solution.py:178
  2.9 0.8 dynamic-slice_convert_fusion
  3.7 0.6 convert_element_type.14.rows_ref
  4.3 0.0 copy-done
  4.3 0.1 broadcast_bitcast_fusion
  4.3 1.4 %fusion.12.mask_ref = f32[2,4096]{1,0:T(2,128)} fusion(s32[1,2,32,128]{3,2,1,0:T(8,128)S(1)} %broadcast_bitcast_fusion, s32[4096]{0:T(1024)} %param.10), kind=kLoop, calls=%fused_computation.40 | loop fusion | flops 16384 | bytes 81920 | tf_op jit(solution)/shard_map/convert_element_type | solution.py:171
  5.7 76.0 %shard_map.64 = f32[4,8192]{1,0:T(4,128)} custom-call(s32[8192]{0:T(1024)} %get-tuple-element.8.tile_idx, s32[8192]{0:T(1024)} %get-tuple-element.7.sign_idx, bf16[4,1024,4096]{2,1,0:T(8,128)(2,1)} %x_ref.1, bf16[4,1024,256]{2,1,0:T(8,128)(2,1)} %d_ref.1, f32[64,128]{1,0:T(8,128)} %fusion.13.factor_ref, f32[2,4096]{1,0:T(2,128)} %fusion.12.mask_ref, ...), custom_call_target="tpu_custom_call" | custom-call | tf_op jit(solution)/shard_map/pallas_call | solution.py:133
  81.7 0.9 slice_select_fusion
  82.6 0.6 collective-permute-start
  83.2 0.9 collective-permute-done
  84.1 0.9 select_add_fusion
  85.0 2.9 %collective-permute-start.1 = (f32[4,4096]{1,0:T(4,128)S(1)}, f32[4,4096]{1,0:T(4,128)S(1)}, u32[]{:S(2)}, u32[]{:S(2)}) collective-permute-start(f32[4,4096]{1,0:T(4,128)S(1)} %select_add_fusion), channel_id=1, source_target_pairs={{0,2},{1,3},{2,0},{3,1},{4,6},{5,7},{6,4},{7,5},{8,10},{9,11},{10,... | collective-permute-start | bytes 196616 | tf_op jit(solution)/shard_map/ppermute | solution.py:21
  87.9 2.4 %collective-permute-done.1 = f32[4,4096]{1,0:T(4,128)S(1)} collective-permute-done((f32[4,4096]{1,0:T(4,128)S(1)}, f32[4,4096]{1,0:T(4,128)S(1)}, u32[]{:S(2)}, u32[]{:S(2)}) %collective-permute-start.1) | collective-permute-done | bytes 65568 | tf_op jit(solution)/shard_map/ppermute | solution.py:21
  90.4 2.0 %collective-permute-start.2 = (f32[4,4096]{1,0:T(4,128)S(1)}, f32[4,4096]{1,0:T(4,128)S(1)}, u32[]{:S(2)}, u32[]{:S(2)}) collective-permute-start(f32[4,4096]{1,0:T(4,128)S(1)} %add.61), channel_id=1, source_target_pairs={{0,4},{1,5},{2,6},{3,7},{4,0},{5,1},{6,2},{7,3},{8,12},{9,13},{10,... | collective-permute-start | bytes 196616 | tf_op jit(solution)/shard_map/ppermute | solution.py:21
  92.3 2.3 %collective-permute-done.2 = f32[4,4096]{1,0:T(4,128)S(1)} collective-permute-done((f32[4,4096]{1,0:T(4,128)S(1)}, f32[4,4096]{1,0:T(4,128)S(1)}, u32[]{:S(2)}, u32[]{:S(2)}) %collective-permute-start.2) | collective-permute-done | bytes 65568 | tf_op jit(solution)/shard_map/ppermute | solution.py:21
  94.7 3.0 %collective-permute-start.3 = (f32[4,4096]{1,0:T(4,128)S(1)}, f32[4,4096]{1,0:T(4,128)S(1)}, u32[]{:S(2)}, u32[]{:S(2)}) collective-permute-start(f32[4,4096]{1,0:T(4,128)S(1)} %add.62), channel_id=1, source_target_pairs={{0,8},{1,9},{2,10},{3,11},{4,12},{5,13},{6,14},{7,15},{8,0},{9,1},... | collective-permute-start | bytes 196616 | tf_op jit(solution)/shard_map/ppermute | solution.py:21
  97.7 2.2 %collective-permute-done.3 = f32[4,4096]{1,0:T(4,128)S(1)} collective-permute-done((f32[4,4096]{1,0:T(4,128)S(1)}, f32[4,4096]{1,0:T(4,128)S(1)}, u32[]{:S(2)}, u32[]{:S(2)}) %collective-permute-start.3) | collective-permute-done | bytes 65568 | tf_op jit(solution)/shard_map/ppermute | solution.py:21
  100.0 0.1 collective-permute-start.4
  100.0 1.2 %collective-permute-done.4 = f32[4,4096]{1,0:T(4,128)S(1)} collective-permute-done((f32[4,4096]{1,0:T(4,128)S(1)}, f32[4,4096]{1,0:T(4,128)S(1)}, u32[]{:S(2)}, u32[]{:S(2)}) %collective-permute-start.4) | collective-permute-done | bytes 65568 | tf_op jit(solution)/shard_map/ppermute | solution.py:21
  101.3 0.7 pad_maximum_fusion
  (5 shorter events, 0.1 us)
Async XLA Ops:
  0.0 4.3 %copy-start = (s32[32,32]{1,0:T(8,128)S(1)}, s32[32,32]{1,0:T(8,128)}, u32[]{:S(2)}) copy-start(s32[32,32]{1,0:T(8,128)} %param.8) | copy-start | bytes 12292
  82.6 1.5 %collective-permute-start = (f32[4,4096]{1,0:T(4,128)S(1)}, f32[4,4096]{1,0:T(4,128)S(1)}, u32[]{:S(2)}, u32[]{:S(2)}) collective-permute-start(f32[4,4096]{1,0:T(4,128)S(1)} %slice_select_fusion), channel_id=1, source_target_pairs={{0,1},{1,0},{2,3},{3,2},{4,5},{5,4},{6,7},{7,6},{8,9},{9,8},{10,11... | collective-permute-start | bytes 196616 | tf_op jit(solution)/shard_map/ppermute | solution.py:21
  85.0 5.3 %collective-permute-start.1 = (f32[4,4096]{1,0:T(4,128)S(1)}, f32[4,4096]{1,0:T(4,128)S(1)}, u32[]{:S(2)}, u32[]{:S(2)}) collective-permute-start(f32[4,4096]{1,0:T(4,128)S(1)} %select_add_fusion), channel_id=1, source_target_pairs={{0,2},{1,3},{2,0},{3,1},{4,6},{5,7},{6,4},{7,5},{8,10},{9,11},{10,... | collective-permute-start | bytes 196616 | tf_op jit(solution)/shard_map/ppermute | solution.py:21
  90.4 4.3 %collective-permute-start.2 = (f32[4,4096]{1,0:T(4,128)S(1)}, f32[4,4096]{1,0:T(4,128)S(1)}, u32[]{:S(2)}, u32[]{:S(2)}) collective-permute-start(f32[4,4096]{1,0:T(4,128)S(1)} %add.61), channel_id=1, source_target_pairs={{0,4},{1,5},{2,6},{3,7},{4,0},{5,1},{6,2},{7,3},{8,12},{9,13},{10,... | collective-permute-start | bytes 196616 | tf_op jit(solution)/shard_map/ppermute | solution.py:21
  94.7 5.2 %collective-permute-start.3 = (f32[4,4096]{1,0:T(4,128)S(1)}, f32[4,4096]{1,0:T(4,128)S(1)}, u32[]{:S(2)}, u32[]{:S(2)}) collective-permute-start(f32[4,4096]{1,0:T(4,128)S(1)} %add.62), channel_id=1, source_target_pairs={{0,8},{1,9},{2,10},{3,11},{4,12},{5,13},{6,14},{7,15},{8,0},{9,1},... | collective-permute-start | bytes 196616 | tf_op jit(solution)/shard_map/ppermute | solution.py:21
  100.0 1.3 %collective-permute-start.4 = (f32[4,4096]{1,0:T(4,128)S(1)}, f32[4,4096]{1,0:T(4,128)S(1)}, u32[]{:S(2)}, u32[]{:S(2)}) collective-permute-start(f32[4,4096]{1,0:T(4,128)S(1)} %add.63), channel_id=1, source_target_pairs={{0,1},{1,0},{2,3},{3,2},{4,5},{5,4},{6,7},{7,6},{8,9},{9,8},{10,11... | collective-permute-start | bytes 196616 | tf_op jit(solution)/shard_map/ppermute | solution.py:21

commit v2 on v0

v2 whole, which is shorter than its diff:
```python
import functools
import math

import jax
import jax.numpy as jnp
from jax import lax
from jax.experimental import pallas as pl
from jax.experimental.pallas import tpu as pltpu
from jax.sharding import PartitionSpec as P

BLK = 128
LANES = 128
SUBLANES = 8
AT_ONCE = 8
PARTS = 4
PAD = 8
VMEM_LIMIT = 62 * 2**20


def partner(value, axis, apart):
    mask = 2**apart
    pairs = [(source, source ^ mask) for source in range(lax.axis_size(axis))]
    return lax.ppermute(value, axis, pairs)


def parity(ids):
    for shift in (8, 4, 2, 1):
        ids = ids ^ (ids >> shift)
    return ids & 1


def iota(shape, dim):
    return lax.broadcasted_iota(jnp.int32, shape, dim)


def aligned(index, unit):
    return pl.multiple_of(index * unit, unit)


def butterfly(tiles):
    half = 1
    while half < len(tiles):
        tiles = [
            tiles[q] + tiles[q + half] if q & half == 0 else tiles[q - half] - tiles[q]
            for q in range(len(tiles))
        ]
        half *= 2
    return tiles


def sketch_kernel(
    scale, pattern, x_hbm, d_hbm, cols_ref, rows_ref, signs_ref, mine_ref, other_ref,
    x_ref, d_ref, dt_ref, had_ref, flip_ref, idx_ref, t_ref, x_sem, d_sem, idx_sem,
    idx_smem, listed,
):
    examples, tokens, width = x_hbm.shape
    rows = d_hbm.shape[2]
    n_cols = width // LANES
    bands = dt_ref.shape[0] // examples
    band = rows // bands
    n_blocks = bands * n_cols
    block_rows = band * examples
    n_kept = cols_ref.shape[0] * LANES
    per_vreg = SUBLANES // examples
    me = lax.axis_index("feat")
    step = tokens // PARTS

    def x_copy(example, part):
        where = pl.ds(part * step, step)
        slot = example % 2
        return pltpu.make_async_copy(
            x_hbm.at[example, where], x_ref.at[slot, where], x_sem.at[slot, part]
        )

    d_copy = pltpu.make_async_copy(d_hbm, d_ref, d_sem)
    d_copy.start()
    for example in range(min(2, examples)):
        for part in range(PARTS):
            x_copy(example, part).start()

    cols = cols_ref[...]
    kept_row, kept_col = cols // width, cols % width
    local = kept_row % rows
    block = local // band * n_cols + kept_col // LANES
    place = iota(cols.shape, 0) % per_vreg
    idx_ref[...] = PAD + (block * band + local % band) * examples - place * examples

    had_ref[...] = (1 - 2 * parity(iota((band, band), 0) & iota((band, band), 1))).astype(
        jnp.bfloat16
    )
    bits = (iota((SUBLANES, LANES), 1) >> iota((SUBLANES, LANES), 0) & 1).astype(jnp.bfloat16)

    def flips(group, carry):
        lane = cols_ref[pl.ds(group, 1), :] % LANES
        mine = (lane >> iota((SUBLANES, LANES), 0) & 1).astype(jnp.bfloat16)
        shared = lax.dot_general(
            mine, bits, (((0,), (0,)), ((), ())), preferred_element_type=jnp.float32
        )
        odd = (shared.astype(jnp.int32) & 1).astype(jnp.float32)
        flip_ref[pl.ds(aligned(group, LANES), LANES), :] = 1.0 - 2.0 * odd
        return carry

    lax.fori_loop(0, n_kept // LANES, flips, 0)

    idx_copy = pltpu.make_async_copy(idx_ref, idx_smem, idx_sem)
    idx_copy.start()

    first = me * rows // BLK

    def listing(b, count):
        def one(q, count):
            listed[count] = b * n_cols + q
            return count + pattern[first + b, q]

        count = lax.fori_loop(0, n_cols, one, count)
        listed[count] = n_blocks
        return count + count % 2

    count = 0
    for b in range(bands):
        count = listing(b, count)
    for extra in range(AT_ONCE):
        listed[count + extra] = n_blocks
    n_steps = (count + AT_ONCE - 1) // AT_ONCE

    def clear(i, carry):
        @pl.when(pattern[first + i // n_cols, i % n_cols] == 0)
        def _():
            here = pl.ds(pl.multiple_of(PAD + i * block_rows, SUBLANES), block_rows)
            t_ref[here, :] = jnp.zeros((block_rows, LANES), jnp.float32)

        return carry

    lax.fori_loop(0, n_blocks, clear, 0)

    d_copy.wait()
    for example in range(examples):
        turned = (d_ref[example] * rows_ref[...]).T
        for b in range(bands):
            dt_ref[example * bands + b] = turned[b * band : (b + 1) * band, :]

    def one_example(example, carry):
        slot = example % 2
        for part in range(PARTS):
            x_copy(example, part).wait()

        def some_blocks(s, carry):
            ids = [listed[s * AT_ONCE + i] for i in range(AT_ONCE)]
            grads, signed, sums = [], [], []
            for i in range(0, AT_ONCE, 2):
                b = ids[i] // n_cols % bands
                acts = [
                    x_ref[slot, :, pl.ds(aligned(ids[i + k] % n_cols, LANES), LANES)]
                    for k in range(2)
                ]
                grads.append(
                    jnp.dot(
                        dt_ref[example * bands + b],
                        jnp.concatenate(acts, axis=1),
                        preferred_element_type=jnp.float32,
                    )
                )
            for i in range(0, AT_ONCE, 2):
                flip = jnp.concatenate(
                    [signs_ref[pl.ds(ids[i + k] % n_cols, 1), :] for k in range(2)], axis=1
                ).astype(jnp.float32)
                signed.append((grads[i // 2] * flip).astype(jnp.bfloat16))
            for i in range(0, AT_ONCE, 2):
                sums.append(
                    jnp.dot(had_ref[...], signed[i // 2], preferred_element_type=jnp.float32)
                )
            for i in range(AT_ONCE):
                start = PAD + ids[i] * block_rows + example
                half = slice(i % 2 * LANES, (i % 2 + 1) * LANES)
                t_ref[pl.ds(start, band, stride=examples), :] = sums[i // 2][:, half]
            return carry

        lax.fori_loop(0, n_steps, some_blocks, 0)

        @pl.when(example + 2 < examples)
        def _():
            for part in range(PARTS):
                x_copy(example + 2, part).start()

        return carry

    lax.fori_loop(0, examples, one_example, 0)

    def across(r, carry):
        def here(i):
            start = PAD + i * block_rows + r * SUBLANES
            return pl.ds(pl.multiple_of(start, SUBLANES), SUBLANES)

        for b in range(bands):
            tiles = butterfly([t_ref[here(b * n_cols + q), :] for q in range(n_cols)])
            if b % 2 == 0:
                for q in range(n_cols):
                    t_ref[here(b * n_cols + q), :] = tiles[q]
            else:
                for q in range(n_cols):
                    low = t_ref[here((b - 1) * n_cols + q), :]
                    t_ref[here((b - 1) * n_cols + q), :] = low + tiles[q]
                    t_ref[here(b * n_cols + q), :] = low - tiles[q]
        return carry

    lax.fori_loop(0, block_rows // SUBLANES, across, 0)

    idx_copy.wait()
    lane = iota((SUBLANES, LANES), 1)
    spot = iota((SUBLANES, LANES), 0) // examples
    n_groups = n_kept // LANES // per_vreg
    half = n_groups // 2

    def sample(out_ref, base):
        def body(i, carry):
            group = base + i
            found = jnp.zeros((SUBLANES, LANES), jnp.float32)
            for u in range(LANES):
                term = None
                for p in range(per_vreg):
                    line = group * per_vreg + p
                    tile = t_ref[pl.ds(idx_smem[line, u], SUBLANES), :]
                    flip = flip_ref[pl.ds(line * LANES + u, SUBLANES, stride=0), :]
                    tile = tile * flip
                    term = tile if p == 0 else jnp.where(spot == p, tile, term)
                total = jnp.sum(term, axis=1, keepdims=True)
                found = jnp.where(lane == u, total, found)
            for p in range(per_vreg):
                line = group * per_vreg + p
                top = cols_ref[pl.ds(line, 1), :] // width // rows
                factor = (1 - 2 * parity(top & me)).astype(jnp.float32) * scale
                there = pl.ds(aligned(i * per_vreg + p, LANES), LANES)
                out_ref[:, there] = found[p * examples : (p + 1) * examples] * factor
            return carry

        lax.fori_loop(0, half, body, 0)

    sample(other_ref, (1 - me % 2) * half)
    sample(mine_ref, me % 2 * half)


def sketch(x_acts, delta, pattern, sign_rows, col_signs, cols):
    examples, tokens, width = x_acts.shape
    rows = delta.shape[2]
    n_kept = cols.shape[0]
    bands = max(rows // BLK, 1)
    band = rows // bands
    n_blocks = bands * width // LANES
    hbm = pl.BlockSpec(memory_space=pl.ANY)
    vmem = pl.BlockSpec(memory_space=pltpu.VMEM)
    scale = 1.0 / (tokens * math.sqrt(n_kept))
    part = jax.ShapeDtypeStruct((examples, n_kept // 2), jnp.float32)
    return pl.pallas_call(
        functools.partial(sketch_kernel, scale),
        out_shape=(part, part),
        in_specs=[pl.BlockSpec(memory_space=pltpu.SMEM), hbm, hbm, vmem, vmem, vmem],
        out_specs=(vmem, vmem),
        scratch_shapes=[
            pltpu.VMEM((2, tokens, width), jnp.bfloat16),
            pltpu.VMEM((examples, tokens, rows), jnp.bfloat16),
            pltpu.VMEM((examples * bands, band, tokens), jnp.bfloat16),
            pltpu.VMEM((band, band), jnp.bfloat16),
            pltpu.VMEM((n_kept, LANES), jnp.float32),
            pltpu.VMEM((n_kept // LANES, LANES), jnp.int32),
            pltpu.VMEM((PAD + (n_blocks + 1) * band * examples, LANES), jnp.float32),
            pltpu.SemaphoreType.DMA((2, PARTS)),
            pltpu.SemaphoreType.DMA,
            pltpu.SemaphoreType.DMA,
            pltpu.SMEM((n_kept // LANES, LANES), jnp.int32),
            pltpu.SMEM((n_blocks + 2 * bands + AT_ONCE,), jnp.int32),
        ],
        compiler_params=pltpu.CompilerParams(vmem_limit_bytes=VMEM_LIMIT),
    )(
        pattern, x_acts, delta, cols.reshape(-1, LANES), sign_rows,
        col_signs.reshape(-1, LANES),
    )


def per_device(x_acts, delta, pattern, row_signs, col_signs, cols):
    rows = delta.shape[2]
    feat = lax.axis_size("feat")
    me = lax.axis_index("feat")
    sign_rows = lax.dynamic_slice_in_dim(row_signs, me * rows, rows, 0)
    sign_rows = sign_rows[None].astype(jnp.bfloat16)

    mine, other = sketch(x_acts, delta, pattern, sign_rows, col_signs, cols)

    bits = max(feat - 1, 0).bit_length()
    mine = mine + partner(other, "feat", 0)
    for bit in range(1, bits):
        mine = mine + partner(mine, "feat", bit)
    back = partner(mine, "feat", 0)
    low = me % 2 == 0
    return jnp.concatenate([jnp.where(low, mine, back), jnp.where(low, back, mine)], axis=1)


def solution(mesh):
    placed = (P("grp", None, None), P("grp", None, "feat"), P(), P(), P(), P())
    return jax.shard_map(
        per_device, mesh=mesh, in_specs=placed, out_specs=P("grp", None), check_vma=False
    )
```

time: 285 us -> 77.9 us (0.27)
  local copies, waits for them, and re-layouts: 123 us -> 0.55 us
  other arithmetic: 68.6 us -> 2.39 us
  matrix products: 57 us -> 0 us
  Pallas kernels: 0 us -> 48.9 us
  blocking collectives: 22 us -> 0 us
  waiting for transfers between devices: 2.92 us -> 13.1 us
  starting transfers between devices: 9.8 us -> 13.2 us
    dot_general x4 -> x0, matrix products: 57 us -> none  [the longest x1 21.4 us: column_section(): jnp.einsum('erqk,qp->pker', section, hadamard(high_width), precision=lax....]
    gather x2 -> x0, local copies, waits for them, and re-layouts: 55.5 us -> none  [the longest x1 49.4 us: kept_entries(): picked = jnp.take(section, cols % width_in, axis=0)]
    pallas_call x0 -> x1, Pallas kernels: none -> 48.9 us  [sketch(): pl.pallas_call(functools.partial(sketch_kernel, scale), out_shape=(part,...]
    unnamed x2 -> x0, other arithmetic: 43.8 us -> none
    unnamed x12 -> x0, local copies, waits for them, and re-layouts: 42.9 us -> none
    all_gather x1 -> x0, blocking collectives: 22 us -> none  [per_device(): gathered = lax.all_gather(mine[None], 'feat', axis=0, tiled=True)]
    reshape x2 -> x0, local copies, waits for them, and re-layouts: 21.3 us -> none  [the longest x1 16.5 us: column_section(): return section.reshape(width_in, examples, rows_here)]
    dot_general x1 -> x0, other arithmetic: 21.1 us -> none  [kept_entries(): jnp.einsum('ker,rk->ek', picked, weight, precision=lax.Precision.HIGHEST)]
  transfers between devices with their start and end apart: 3 -> 5, of which waited for: 2 -> 5; matrix products, arithmetic and copies ran while one was open for 32% -> 0% of each run, Pallas kernels for 0% -> 0%
where the time goes in v2:
time: 77.9 us; the launch traced here: 78.1 us
  Pallas kernels  48.9 us (63%)
  starting transfers between devices  13.2 us (17%)
  waiting for transfers between devices  13.1 us (17%)
  other arithmetic  2.39 us (3%)
    pallas_call x1, Pallas kernels, sketch(): pl.pallas_call(functools.partial(sketch_kernel, scale), out_shape=(part,...  48.9 us
    ppermute x5, starting transfers between devices, partner(): return lax.ppermute(value, axis, pairs)  13.2 us
    ppermute x5, waiting for transfers between devices, partner(): return lax.ppermute(value, axis, pairs)  13.1 us
  transfers between devices with their start and end apart: 5, of which 5 were waited for; matrix products, arithmetic and copies ran while one was open for 0% of the time, Pallas kernels for 0%

profile of v2, /device:TPU:0, one launch (start us, length us, event | category | flops | bytes accessed | tf_op | source)
XLA Modules:
  0.0 78.1 jit_solution(17391294403696736792)
XLA Ops:
  0.0 0.8 dynamic-slice_convert_fusion
  0.8 0.6 convert_element_type.6.rows_ref
  1.3 48.9 %shard_map.64 = (f32[4,4096]{1,0:T(4,128)}, f32[4,4096]{1,0:T(4,128)}) custom-call(s32[32,32]{1,0:T(8,128)} %pattern.1, bf16[4,1024,4096]{2,1,0:T(8,128)(2,1)} %x_hbm.1, bf16[4,1024,256]{2,1,0:T(8,128)(2,1)} %d_hbm.1, s32[64,128]{1,0:T(8,128)} %bitcast.2, bf16[1,256]{1,0:T(2,128)(2,1)} %convert_element_type.6.rows_ref, s32[32,128]{1,0:T(8,128)} %bitcast.3), custom_call_target="tpu_custom_call" | custom-call | tf_op jit(solution)/shard_map/pallas_call | solution.py:253
  50.2 0.6 collective-permute-start
  50.7 1.1 %collective-permute-done = f32[4,4096]{1,0:T(4,128)S(1)} collective-permute-done((f32[4,4096]{1,0:T(4,128)}, f32[4,4096]{1,0:T(4,128)S(1)}, u32[]{:S(2)}, u32[]{:S(2)}) %collective-permute-start) | collective-permute-done | bytes 65568 | tf_op jit(solution)/shard_map/ppermute | solution.py:23
  51.8 0.9 %add.21 = f32[4,4096]{1,0:T(4,128)S(1)} add(f32[4,4096]{1,0:T(4,128)} %get-tuple-element.7, f32[4,4096]{1,0:T(4,128)S(1)} %collective-permute-done) | non-fusion elementwise | flops 16384 | bytes 196608 | tf_op jit(solution)/shard_map/add | solution.py:289
  52.7 10.6 %collective-permute-start.1 = (f32[4,4096]{1,0:T(4,128)S(1)}, f32[4,4096]{1,0:T(4,128)S(1)}, u32[]{:S(2)}, u32[]{:S(2)}) collective-permute-start(f32[4,4096]{1,0:T(4,128)S(1)} %add.21), channel_id=1, source_target_pairs={{0,2},{1,3},{2,0},{3,1},{4,6},{5,7},{6,4},{7,5},{8,10},{9,11},{10,... | collective-permute-start | bytes 196616 | tf_op jit(solution)/shard_map/ppermute | solution.py:23
  63.3 2.4 %collective-permute-done.1 = f32[4,4096]{1,0:T(4,128)S(1)} collective-permute-done((f32[4,4096]{1,0:T(4,128)S(1)}, f32[4,4096]{1,0:T(4,128)S(1)}, u32[]{:S(2)}, u32[]{:S(2)}) %collective-permute-start.1) | collective-permute-done | bytes 65568 | tf_op jit(solution)/shard_map/ppermute | solution.py:23
  65.7 0.1 collective-permute-start.2
  65.8 4.3 %collective-permute-done.2 = f32[4,4096]{1,0:T(4,128)S(1)} collective-permute-done((f32[4,4096]{1,0:T(4,128)S(1)}, f32[4,4096]{1,0:T(4,128)S(1)}, u32[]{:S(2)}, u32[]{:S(2)}) %collective-permute-start.2) | collective-permute-done | bytes 65568 | tf_op jit(solution)/shard_map/ppermute | solution.py:23
  70.1 1.9 %collective-permute-start.3 = (f32[4,4096]{1,0:T(4,128)S(1)}, f32[4,4096]{1,0:T(4,128)S(1)}, u32[]{:S(2)}, u32[]{:S(2)}) collective-permute-start(f32[4,4096]{1,0:T(4,128)S(1)} %add.23), channel_id=1, source_target_pairs={{0,8},{1,9},{2,10},{3,11},{4,12},{5,13},{6,14},{7,15},{8,0},{9,1},... | collective-permute-start | bytes 196616 | tf_op jit(solution)/shard_map/ppermute | solution.py:23
  72.0 4.0 %collective-permute-done.3 = f32[4,4096]{1,0:T(4,128)S(1)} collective-permute-done((f32[4,4096]{1,0:T(4,128)S(1)}, f32[4,4096]{1,0:T(4,128)S(1)}, u32[]{:S(2)}, u32[]{:S(2)}) %collective-permute-start.3) | collective-permute-done | bytes 65568 | tf_op jit(solution)/shard_map/ppermute | solution.py:23
  76.0 0.1 collective-permute-start.4
  76.1 1.2 %collective-permute-done.4 = f32[4,4096]{1,0:T(4,128)S(1)} collective-permute-done((f32[4,4096]{1,0:T(4,128)S(1)}, f32[4,4096]{1,0:T(4,128)S(1)}, u32[]{:S(2)}, u32[]{:S(2)}) %collective-permute-start.4) | collective-permute-done | bytes 65568 | tf_op jit(solution)/shard_map/ppermute | solution.py:23
  77.4 0.7 pad_maximum_fusion
  (4 shorter events, 0.1 us)
Async XLA Ops:
  50.2 1.7 %collective-permute-start = (f32[4,4096]{1,0:T(4,128)}, f32[4,4096]{1,0:T(4,128)S(1)}, u32[]{:S(2)}, u32[]{:S(2)}) collective-permute-start(f32[4,4096]{1,0:T(4,128)} %get-tuple-element.8), channel_id=1, source_target_pairs={{0,1},{1,0},{2,3},{3,2},{4,5},{5,4},{6,7},{7,6},{8,9},{9,8},{10,11... | collective-permute-start | bytes 196616 | tf_op jit(solution)/shard_map/ppermute | solution.py:23
  52.7 13.0 %collective-permute-start.1 = (f32[4,4096]{1,0:T(4,128)S(1)}, f32[4,4096]{1,0:T(4,128)S(1)}, u32[]{:S(2)}, u32[]{:S(2)}) collective-permute-start(f32[4,4096]{1,0:T(4,128)S(1)} %add.21), channel_id=1, source_target_pairs={{0,2},{1,3},{2,0},{3,1},{4,6},{5,7},{6,4},{7,5},{8,10},{9,11},{10,... | collective-permute-start | bytes 196616 | tf_op jit(solution)/shard_map/ppermute | solution.py:23
  65.7 4.3 %collective-permute-start.2 = (f32[4,4096]{1,0:T(4,128)S(1)}, f32[4,4096]{1,0:T(4,128)S(1)}, u32[]{:S(2)}, u32[]{:S(2)}) collective-permute-start(f32[4,4096]{1,0:T(4,128)S(1)} %add.22), channel_id=1, source_target_pairs={{0,4},{1,5},{2,6},{3,7},{4,0},{5,1},{6,2},{7,3},{8,12},{9,13},{10,... | collective-permute-start | bytes 196616 | tf_op jit(solution)/shard_map/ppermute | solution.py:23
  70.1 5.9 %collective-permute-start.3 = (f32[4,4096]{1,0:T(4,128)S(1)}, f32[4,4096]{1,0:T(4,128)S(1)}, u32[]{:S(2)}, u32[]{:S(2)}) collective-permute-start(f32[4,4096]{1,0:T(4,128)S(1)} %add.23), channel_id=1, source_target_pairs={{0,8},{1,9},{2,10},{3,11},{4,12},{5,13},{6,14},{7,15},{8,0},{9,1},... | collective-permute-start | bytes 196616 | tf_op jit(solution)/shard_map/ppermute | solution.py:23
  76.0 1.3 %collective-permute-start.4 = (f32[4,4096]{1,0:T(4,128)S(1)}, f32[4,4096]{1,0:T(4,128)S(1)}, u32[]{:S(2)}, u32[]{:S(2)}) collective-permute-start(f32[4,4096]{1,0:T(4,128)S(1)} %add.24), channel_id=1, source_target_pairs={{0,1},{1,0},{2,3},{3,2},{4,5},{5,4},{6,7},{7,6},{8,9},{9,8},{10,11... | collective-permute-start | bytes 196616 | tf_op jit(solution)/shard_map/ppermute | solution.py:23
